TPU v7x, 32 devices: a whole 2x2x4 slice. The times are simulated.
32 devices in a mesh: dp: 4 (over z), adapter: 8 (over y, x, core).
Axes of the slice: x: 2, y: 2, z: 4, core: 2. Of those that a mesh axis runs over, the one named last changes fastest.
Arguments:
- states: bfloat16 [2, 1024, 8192], P(None, ('dp', 'adapter')), may hold values from -6 to 6
- request_slot_index: int32 [2, 1024, 1], P(None, ('dp', 'adapter')), may hold values from 0 to 7; in each aligned block of 32 rows (0 to 31, 32 to 63, ..., all dimensions but the last counted through in order) at most 8 rows name the same one
- down_weights: bfloat16 [32, 64, 8192], P(('dp', 'adapter')), may hold values from -0.0625 to 0.0625
- up_weights: bfloat16 [32, 64, 8192], P(('dp', 'adapter')), may hold values from -0.75 to 0.75
- active_adapter_owner: int32 [2, 8], replicated, may hold values from 0 to 3
Outputs:
- delta: bfloat16 [2, 1024, 8192], P(None, ('dp', 'adapter'))
Inputs may be any that keep to these rules, and one draw needn't show every extreme that they name: `request_slot_index`: within the rows of one device at one step (aligned blocks of 32 rows), no column is named by more than 8 rows, a bound that some block reaches.
All inputs are finite; a program needn't handle non-finite values.
Results may differ from a plain program's by a relative error of at most 0.0049.
Values may be sent and summed in bfloat16 or wider, within the bound.
A program may use at most 64 MiB of HBM per device.

v0:
```python
import jax
import jax.numpy as jnp
from jax import lax
from jax.sharding import PartitionSpec as P


def from_root(array, axis, root):
    mine = lax.axis_index(axis) == root
    return lax.psum(jnp.where(mine, array, jnp.zeros_like(array)), axis)


def slot_matrix(column_ids, columns, capacity):
    hits = (column_ids[:, None] == jnp.arange(columns, dtype=jnp.int32)[None, :]).astype(jnp.int32)
    slot_rank = jnp.sum(jnp.cumsum(hits, axis=0) * hits, axis=1) - 1
    target = column_ids * capacity + slot_rank
    return (target[:, None] == jnp.arange(columns * capacity, dtype=jnp.int32)[None, :]).astype(
        jnp.bfloat16
    )


def project(arrived, stack_down, stack_up):
    low_rank = jnp.einsum(
        "scnd,srd->scnr", arrived, stack_down, preferred_element_type=jnp.float32
    ).astype(jnp.bfloat16)
    return jnp.einsum(
        "scnr,srd->scnd", low_rank, stack_up, preferred_element_type=jnp.float32
    ).astype(jnp.bfloat16)


def serve_one(arrived, stack_down, stack_up):
    result = project(arrived, stack_down, stack_up)
    return lax.all_to_all(result, "adapter", split_axis=1, concat_axis=1, tiled=True)


def body(states, request_slot_index, down_weights, up_weights, active_adapter_owner):
    step_count = states.shape[0]
    rows_dev = states.shape[1]
    model_width = states.shape[2]
    columns = lax.axis_size("adapter")
    column_index = lax.axis_index("adapter")
    capacity = max(2, 2 * rows_dev // columns)
    slot_count = columns * capacity
    downs = []
    uppers = []
    for step_index in range(step_count):
        owner_leader = active_adapter_owner[step_index, column_index]
        got_down, got_up = (
            from_root(down_weights[0], "dp", owner_leader),
            from_root(up_weights[0], "dp", owner_leader),
        )
        downs.append(got_down)
        uppers.append(got_up)
    stack_down = jnp.stack(downs)
    stack_up = jnp.stack(uppers)
    placements = []
    outgoing_list = []
    for step_index in range(step_count):
        placement = slot_matrix(request_slot_index[step_index, :, 0], columns, capacity)
        placements.append(placement)
        packed = lax.dot_general(
            placement,
            states[step_index],
            (((0,), (0,)), ((), ())),
            preferred_element_type=jnp.float32,
        )
        outgoing_list.append(packed.astype(jnp.bfloat16).reshape(columns, capacity, model_width))
    outgoing = jnp.stack(outgoing_list)
    returned_list = []
    for step_index in range(step_count):
        returned_list.append(
            serve_one(
                lax.all_to_all(
                    outgoing[step_index : step_index + 1],
                    "adapter",
                    split_axis=1,
                    concat_axis=1,
                    tiled=True,
                ),
                stack_down=stack_down[step_index : step_index + 1],
                stack_up=stack_up[step_index : step_index + 1],
            )
        )
    returned_rows = jnp.concatenate(returned_list, axis=0)
    delta_list = []
    for step_index in range(step_count):
        flat_rows = returned_rows[step_index].reshape(slot_count, model_width)
        delta_list.append(
            jnp.dot(placements[step_index], flat_rows, preferred_element_type=jnp.float32).astype(
                jnp.bfloat16
            )
        )
    return jnp.stack(delta_list)


def solution(mesh):
    return jax.shard_map(
        body,
        mesh=mesh,
        in_specs=(
            P(None, ("dp", "adapter"), None),
            P(None, ("dp", "adapter"), None),
            P(("dp", "adapter"), None, None),
            P(("dp", "adapter"), None, None),
            P(),
        ),
        out_specs=P(None, ("dp", "adapter"), None),
        check_vma=False,
    )
```

profile of v0, /device:TPU:0, one launch (start us, length us, event | category | flops | bytes accessed | tf_op | source)
XLA Modules:
  0.0 222.1 jit_solution(10519682711103507936)
XLA Ops:
  6.5 1.4 constant_dynamic-slice_fusion.1
  9.3 3.7 %select_bitcast_fusion.2 = (bf16[64,8192]{1,0:T(8,128)(2,1)}, bf16[64,8192]{1,0:T(8,128)(2,1)}, bf16[64,8192]{1,0:T(8,128)(2,1)}, bf16[64,8192]{1,0:T(8,128)(2,1)}) fusion(bf16[1,64,8192]{2,1,0:T(8,128)(2,1)} %param.8, pred[]{:T(512)S(6)} %eq.66, pred[]{:T(512)S(6)} %eq.73, bf16[1,64,8192]{2,1,0:T(8,128)(2,1)} %param.7), kind=kLoop, calls=%fused_computation.25 | loop fusion | flops 2097152 | bytes 6291458 | tf_op jit(solution)/shard_map/jit(_where)/select_n | solution.py:9
  13.0 0.7 copy-done.2
  13.6 0.1 fusion.23
  13.7 0.1 reduce_window_sum.17
  13.8 0.1 fusion.22
  13.8 0.1 reduce_window_sum.18
  13.9 0.2 select_reduce_fusion
  14.1 0.1 copy-done
  14.2 1.6 fusion
  15.8 5.2 %all-to-all-start = ((bf16[1,8,8,8192]{3,2,0,1:T(8,128)(2,1)}), bf16[1,8,8,8192]{3,2,0,1:T(8,128)(2,1)S(1)}, u32[]{:S(2)}, u32[]{:S(2)}) async-start(bf16[1,8,8,8192]{3,2,0,1:T(8,128)(2,1)} %fusion), calls=%async_computation | async-start | bytes 2097152 | tf_op jit(solution)/shard_map/all_to_all | solution.py:72
  21.0 1.6 fusion.2
  22.5 13.8 %all-to-all-done = bf16[1,8,8,8192]{3,2,0,1:T(8,128)(2,1)S(1)} async-done(((bf16[1,8,8,8192]{3,2,0,1:T(8,128)(2,1)}), bf16[1,8,8,8192]{3,2,0,1:T(8,128)(2,1)S(1)}, u32[]{:S(2)}, u32[]{:S(2)}) %all-to-all-start) | async-done | bytes 1048608 | tf_op jit(solution)/shard_map/all_to_all | solution.py:72
  36.4 3.6 %all-to-all-start.2 = ((bf16[1,8,8,8192]{3,2,0,1:T(8,128)(2,1)}), bf16[1,8,8,8192]{3,2,0,1:T(8,128)(2,1)S(1)}, u32[]{:S(2)}, u32[]{:S(2)}) async-start(bf16[1,8,8,8192]{3,2,0,1:T(8,128)(2,1)} %fusion.2), calls=%async_computation.2 | async-start | bytes 2097152 | tf_op jit(solution)/shard_map/all_to_all | solution.py:72
  39.9 131.9 %all-reduce.3.cloned.1.call-done = (bf16[64,8192]{1,0:T(8,128)(2,1)}, bf16[64,8192]{1,0:T(8,128)(2,1)}, bf16[64,8192]{1,0:T(8,128)(2,1)}, bf16[64,8192]{1,0:T(8,128)(2,1)}) async-done(((bf16[64,8192]{1,0:T(8,128)(2,1)}, bf16[64,8192]{1,0:T(8,128)(2,1)}, bf16[64,8192]{1,0:T(8,128)(2,1)}, bf16[64,8192]{1,0:T(8,128)(2,1)}), (bf16[64,8192]{1,0:T(8,128)(2,1)}, bf16[64,8192]{1,0:T(8,128)(2,1)}, ...) | async-done | bytes 4194320 | tf_op jit(solution)/shard_map/psum | solution.py:9
  171.9 3.8 %fusion.1 = bf16[1,8,8,8192]{3,2,0,1:T(8,128)(2,1)} fusion(bf16[64,8192]{1,0:T(8,128)(2,1)} %get-tuple-element.7, bf16[64,8192]{1,0:T(8,128)(2,1)} %get-tuple-element.8, bf16[1,8,8,8192]{3,2,0,1:T(8,128)(2,1)S(1)} %all-to-all-done), kind=kOutput, calls=%fused_computation.5 | convolution fusion | flops 134746112 | bytes 4194304 | tf_op jit(solution)/shard_map/scnr,srd->scnd/dot_general | solution.py:25
  175.7 3.8 %all-to-all-start.1 = ((bf16[1,8,8,8192]{3,2,0,1:T(8,128)(2,1)}), bf16[1,8,8,8192]{3,2,0,1:T(8,128)(2,1)S(1)}, u32[]{:S(2)}, u32[]{:S(2)}) async-start(bf16[1,8,8,8192]{3,2,0,1:T(8,128)(2,1)} %fusion.1), calls=%async_computation.1 | async-start | bytes 2097152 | tf_op jit(solution)/shard_map/all_to_all | solution.py:32
  179.5 3.5 %fusion.3 = bf16[1,8,8,8192]{3,2,0,1:T(8,128)(2,1)} fusion(bf16[64,8192]{1,0:T(8,128)(2,1)S(1)} %copy-done.1, bf16[64,8192]{1,0:T(8,128)(2,1)} %get-tuple-element.6, bf16[1,8,8,8192]{3,2,0,1:T(8,128)(2,1)S(1)} %all-to-all-done.2), kind=kOutput, calls=%fused_computation.7 | convolution fusion | flops 134746112 | bytes 4194304 | tf_op jit(solution)/shard_map/scnr,srd->scnd/dot_general | solution.py:25
  183.0 11.9 %all-to-all-done.1 = bf16[1,8,8,8192]{3,2,0,1:T(8,128)(2,1)S(1)} async-done(((bf16[1,8,8,8192]{3,2,0,1:T(8,128)(2,1)}), bf16[1,8,8,8192]{3,2,0,1:T(8,128)(2,1)S(1)}, u32[]{:S(2)}, u32[]{:S(2)}) %all-to-all-start.1) | async-done | bytes 1048608 | tf_op jit(solution)/shard_map/all_to_all | solution.py:32
  194.9 3.6 %all-to-all-start.3 = ((bf16[1,8,8,8192]{3,2,0,1:T(8,128)(2,1)}), bf16[1,8,8,8192]{3,2,0,1:T(8,128)(2,1)S(1)}, u32[]{:S(2)}, u32[]{:S(2)}) async-start(bf16[1,8,8,8192]{3,2,0,1:T(8,128)(2,1)} %fusion.3), calls=%async_computation.3 | async-start | bytes 2097152 | tf_op jit(solution)/shard_map/all_to_all | solution.py:32
  198.5 0.4 fusion.4
  198.9 15.0 %all-to-all-done.3 = bf16[1,8,8,8192]{3,2,0,1:T(8,128)(2,1)S(1)} async-done(((bf16[1,8,8,8192]{3,2,0,1:T(8,128)(2,1)}), bf16[1,8,8,8192]{3,2,0,1:T(8,128)(2,1)S(1)}, u32[]{:S(2)}, u32[]{:S(2)}) %all-to-all-start.3) | async-done | bytes 1048608 | tf_op jit(solution)/shard_map/all_to_all | solution.py:32
  213.8 0.3 fusion.5
  214.2 1.1 pad_maximum_fusion
  (9 shorter events, 0.0 us)
Async XLA Ops:
  6.5 165.3 %all-reduce.3.cloned.1.call-start = ((), (), s32[]{:S(2)}) async-start(), calls=%async_computation.4 | async-start | bytes 8388608 | tf_op jit(solution)/shard_map/psum | solution.py:9
  13.0 0.7 copy-start.2
  13.0 1.2 copy-start
  15.8 20.6 %all-to-all-start = ((bf16[1,8,8,8192]{3,2,0,1:T(8,128)(2,1)}), bf16[1,8,8,8192]{3,2,0,1:T(8,128)(2,1)S(1)}, u32[]{:S(2)}, u32[]{:S(2)}) async-start(bf16[1,8,8,8192]{3,2,0,1:T(8,128)(2,1)} %fusion), calls=%async_computation | async-start | bytes 2097152 | tf_op jit(solution)/shard_map/all_to_all | solution.py:72
  36.4 139.3 %all-to-all-start.2 = ((bf16[1,8,8,8192]{3,2,0,1:T(8,128)(2,1)}), bf16[1,8,8,8192]{3,2,0,1:T(8,128)(2,1)S(1)}, u32[]{:S(2)}, u32[]{:S(2)}) async-start(bf16[1,8,8,8192]{3,2,0,1:T(8,128)(2,1)} %fusion.2), calls=%async_computation.2 | async-start | bytes 2097152 | tf_op jit(solution)/shard_map/all_to_all | solution.py:72
  175.7 3.8 %copy-start.1 = (bf16[64,8192]{1,0:T(8,128)(2,1)S(1)}, bf16[64,8192]{1,0:T(8,128)(2,1)}, u32[]{:S(2)}) copy-start(bf16[64,8192]{1,0:T(8,128)(2,1)} %get-tuple-element.5) | copy-start | bytes 3145732
  175.7 19.2 %all-to-all-start.1 = ((bf16[1,8,8,8192]{3,2,0,1:T(8,128)(2,1)}), bf16[1,8,8,8192]{3,2,0,1:T(8,128)(2,1)S(1)}, u32[]{:S(2)}, u32[]{:S(2)}) async-start(bf16[1,8,8,8192]{3,2,0,1:T(8,128)(2,1)} %fusion.1), calls=%async_computation.1 | async-start | bytes 2097152 | tf_op jit(solution)/shard_map/all_to_all | solution.py:32
  194.9 18.9 %all-to-all-start.3 = ((bf16[1,8,8,8192]{3,2,0,1:T(8,128)(2,1)}), bf16[1,8,8,8192]{3,2,0,1:T(8,128)(2,1)S(1)}, u32[]{:S(2)}, u32[]{:S(2)}) async-start(bf16[1,8,8,8192]{3,2,0,1:T(8,128)(2,1)} %fusion.3), calls=%async_computation.3 | async-start | bytes 2097152 | tf_op jit(solution)/shard_map/all_to_all | solution.py:32
Sparse Core Ops, SparseCore 0:
  13.1 158.7 all-reduce.2
where the time goes:
time: 223 us; the launch traced here: 222 us
  waiting for transfers between devices  173 us (78%)
  starting transfers between devices  16.1 us (7%)
  between operations  14.8 us (7%)
  matrix products  11.2 us (5%)
  other arithmetic  5.16 us (2%)
    psum x1, waiting for transfers between devices, from_root(): return lax.psum(jnp.where(mine, array, jnp.zeros_like(array)), axis)  132 us
    all_to_all x2, waiting for transfers between devices, serve_one(): lax.all_to_all(result, 'adapter', split_axis=1, concat_axis=1, tiled=True)  26.9 us
    all_to_all x2, waiting for transfers between devices, body(): lax.all_to_all(outgoing[step_index:step_index + 1], 'adapter', split_axis...  13.9 us
    all_to_all x2, starting transfers between devices, body(): lax.all_to_all(outgoing[step_index:step_index + 1], 'adapter', split_axis...  8.73 us
    all_to_all x2, starting transfers between devices, serve_one(): lax.all_to_all(result, 'adapter', split_axis=1, concat_axis=1, tiled=True)  7.39 us
    dot_general x2, matrix products, project(): jnp.einsum('scnr,srd->scnd', low_rank, stack_up, preferred_element_type=j...  7.33 us
  transfers between devices with their start and end apart: 5, of which 4 were waited for; matrix products, arithmetic and copies ran while one was open for 5% of the time, Pallas kernels for 0%

commit v1 on v0

--- a/solution.py
+++ b/solution.py
@@ -2,6 +2,29 @@
 import jax.numpy as jnp
 from jax import lax
 from jax.sharding import PartitionSpec as P
+
+
+def split_up(value, dim, size):
+    shape = value.shape
+    blocks = value.reshape(*shape[:dim], size, shape[dim] // size, *shape[dim + 1 :])
+    return jnp.moveaxis(blocks, dim, 0)
+
+
+def joined_along(blocks, dim):
+    dims = list(blocks.shape[1:])
+    dims[dim] *= blocks.shape[0]
+    return jnp.moveaxis(blocks, 0, dim).reshape(dims)
+
+
+def rotated_exchange(array, axis, split_dim, concat_dim):
+    devices, index = (lax.axis_size(axis), lax.axis_index(axis))
+    blocks = split_up(array, split_dim, devices)
+    outs = [blocks[index]]
+    for step in range(1, devices):
+        sent = blocks[(index + step) % devices]
+        outs.append(lax.ppermute(sent, axis, [(i, (i + step) % devices) for i in range(devices)]))
+    blocks = jnp.stack(outs)[(index - jnp.arange(devices)) % devices]
+    return joined_along(blocks, concat_dim)
 
 
 def from_root(array, axis, root):
@@ -69,13 +92,7 @@
     for step_index in range(step_count):
         returned_list.append(
             serve_one(
-                lax.all_to_all(
-                    outgoing[step_index : step_index + 1],
-                    "adapter",
-                    split_axis=1,
-                    concat_axis=1,
-                    tiled=True,
-                ),
+                rotated_exchange(outgoing[step_index : step_index + 1], "adapter", 1, 1),
                 stack_down=stack_down[step_index : step_index + 1],
                 stack_up=stack_up[step_index : step_index + 1],
             )

time: 223 us -> 230 us (1.031)
  starting transfers between devices: 16.1 us -> 22.6 us
  local copies, waits for them, and re-layouts: 2.18 us -> 7.4 us
  waiting for transfers between devices: 173 us -> 169 us
    ppermute x0 -> x14, starting transfers between devices: none -> 15.4 us  [rotated_exchange(): lax.ppermute(sent, axis, [(i, (i + step) % devices) for i in range(device...]
    all_to_all x2 -> x0, waiting for transfers between devices: 13.9 us -> none  [body(): lax.all_to_all(outgoing[step_index:step_index + 1], 'adapter', split_axis...]
    all_to_all x2 -> x0, starting transfers between devices: 8.73 us -> none  [body(): lax.all_to_all(outgoing[step_index:step_index + 1], 'adapter', split_axis...]
    ppermute x0 -> x14, waiting for transfers between devices: none -> 7.3 us  [rotated_exchange(): lax.ppermute(sent, axis, [(i, (i + step) % devices) for i in range(device...]
    psum x1, waiting for transfers between devices: 132 us -> 136 us  [from_root(): return lax.psum(jnp.where(mine, array, jnp.zeros_like(array)), axis)]
    unnamed x6 -> x18, local copies, waits for them, and re-layouts: 0.76 us -> 3.18 us
  transfers between devices with their start and end apart: 5 -> 17, of which waited for: 4 -> 8; matrix products, arithmetic and copies ran while one was open for 5% -> 7% of each run, Pallas kernels for 0% -> 0%
where the time goes in v1:
time: 230 us
  waiting for transfers between devices  169 us (73%)
  starting transfers between devices  22.6 us (10%)
  between operations  15 us (7%)
  matrix products  10.5 us (5%)
  local copies, waits for them, and re-layouts  7.4 us (3%)
  other arithmetic  5.52 us (2%)
    psum x1, waiting for transfers between devices, from_root(): return lax.psum(jnp.where(mine, array, jnp.zeros_like(array)), axis)  136 us
    all_to_all x2, waiting for transfers between devices, serve_one(): lax.all_to_all(result, 'adapter', split_axis=1, concat_axis=1, tiled=True)  25.9 us
    ppermute x14, starting transfers between devices, rotated_exchange(): lax.ppermute(sent, axis, [(i, (i + step) % devices) for i in range(device...  15.4 us
    dot_general x2, matrix products, project(): jnp.einsum('scnr,srd->scnd', low_rank, stack_up, preferred_element_type=j...  7.64 us
    ppermute x14, waiting for transfers between devices, rotated_exchange(): lax.ppermute(sent, axis, [(i, (i + step) % devices) for i in range(device...  7.3 us
    all_to_all x2, starting transfers between devices, serve_one(): lax.all_to_all(result, 'adapter', split_axis=1, concat_axis=1, tiled=True)  7.25 us
  transfers between devices with their start and end apart: 17, of which 8 were waited for; matrix products, arithmetic and copies ran while one was open for 7% of the time, Pallas kernels for 0%

profile of v1, /device:TPU:0, one launch (start us, length us, event | category | flops | bytes accessed | tf_op | source)
XLA Modules:
  0.0 229.9 jit_solution(15577797425762858136)
XLA Ops:
  8.3 1.6 fusion.2
  10.0 0.9 dynamic-slice_bitcast_fusion
  11.3 2.5 %collective-permute-start.8 = (bf16[1,1,8,8192]{3,2,1,0:T(8,128)(2,1)}, bf16[1,1,8,8192]{3,2,1,0:T(8,128)(2,1)}, u32[]{:S(2)}, u32[]{:S(2)}) collective-permute-start(bf16[1,1,8,8192]{3,2,1,0:T(8,128)(2,1)} %get-tuple-element.22), channel_id=1, source_target_pairs={{0,2},{1,3},{2,4},{3,5},{4,6},{5,7},{6,0},{7,1},{8,10},{9,11},{10,... | collective-permute-start | bytes 393224 | tf_op jit(solution)/shard_map/ppermute | solution.py:25
  13.9 2.4 %collective-permute-start.9 = (bf16[1,1,8,8192]{3,2,1,0:T(8,128)(2,1)}, bf16[1,1,8,8192]{3,2,1,0:T(8,128)(2,1)S(1)}, u32[]{:S(2)}, u32[]{:S(2)}) collective-permute-start(bf16[1,1,8,8192]{3,2,1,0:T(8,128)(2,1)} %get-tuple-element.21), channel_id=1, source_target_pairs={{0,3},{1,4},{2,5},{3,6},{4,7},{5,0},{6,1},{7,2},{8,11},{9,12},{10,... | collective-permute-start | bytes 393224 | tf_op jit(solution)/shard_map/ppermute | solution.py:25
  18.9 3.3 %select_bitcast_fusion.2 = (bf16[64,8192]{1,0:T(8,128)(2,1)}, bf16[64,8192]{1,0:T(8,128)(2,1)}, bf16[64,8192]{1,0:T(8,128)(2,1)}, bf16[64,8192]{1,0:T(8,128)(2,1)}) fusion(bf16[1,64,8192]{2,1,0:T(8,128)(2,1)S(1)} %copy-done.1, pred[]{:T(512)S(6)} %eq.84, pred[]{:T(512)S(6)} %eq.91, bf16[1,64,8192]{2,1,0:T(8,128)(2,1)} %param.7), kind=kLoop, calls=%fused_computation.25 | loop fusion | flops 2097152 | bytes 6291458 | tf_op jit(solution)/shard_map/jit(_where)/select_n | solution.py:32
  22.2 1.2 copy-done
  24.7 1.5 collective-permute-start.12
  26.2 0.9 bitcast_dynamic-update-slice_fusion.6
  27.1 2.4 %collective-permute-start.13 = (bf16[1,1,8,8192]{3,2,1,0:T(8,128)(2,1)S(1)}, bf16[1,1,8,8192]{3,2,1,0:T(8,128)(2,1)S(1)}, u32[]{:S(2)}, u32[]{:S(2)}) collective-permute-start(bf16[1,1,8,8192]{3,2,1,0:T(8,128)(2,1)S(1)} %get-tuple-element.17), channel_id=1, source_target_pairs={{0,7},{1,0},{2,1},{3,2},{4,3},{5,4},{6,5},{7,6},{8,15},{9,8},{10,9... | collective-permute-start | bytes 393224 | tf_op jit(solution)/shard_map/ppermute | solution.py:25
  29.5 1.0 bitcast_dynamic-update-slice_fusion.5
  31.2 1.4 collective-permute-start.2
  32.7 1.6 collective-permute-start.3
  34.4 2.3 %collective-permute-done = bf16[1,1,8,8192]{3,2,1,0:T(8,128)(2,1)S(1)} collective-permute-done((bf16[1,1,8,8192]{3,2,1,0:T(8,128)(2,1)S(1)}, bf16[1,1,8,8192]{3,2,1,0:T(8,128)(2,1)S(1)}, u32[]{:S(2)}, u32[]{:S(2)}) %collective-permute-start) | collective-permute-done | bytes 131104 | tf_op jit(solution)/shard_map/ppermute | solution.py:25
  36.9 1.0 collective-permute-done.1
  38.0 1.6 collective-permute-start.6
  39.6 3.2 %collective-permute-done.2 = bf16[1,1,8,8192]{3,2,1,0:T(8,128)(2,1)S(1)} collective-permute-done((bf16[1,1,8,8192]{3,2,1,0:T(8,128)(2,1)S(1)}, bf16[1,1,8,8192]{3,2,1,0:T(8,128)(2,1)S(1)}, u32[]{:S(2)}, u32[]{:S(2)}) %collective-permute-start.2) | collective-permute-done | bytes 131104 | tf_op jit(solution)/shard_map/ppermute | solution.py:25
  44.2 135.7 %all-reduce.3.cloned.1.call-done = (bf16[64,8192]{1,0:T(8,128)(2,1)}, bf16[64,8192]{1,0:T(8,128)(2,1)}, bf16[64,8192]{1,0:T(8,128)(2,1)}, bf16[64,8192]{1,0:T(8,128)(2,1)}) async-done(((bf16[64,8192]{1,0:T(8,128)(2,1)}, bf16[64,8192]{1,0:T(8,128)(2,1)}, bf16[64,8192]{1,0:T(8,128)(2,1)}, bf16[64,8192]{1,0:T(8,128)(2,1)}), (bf16[64,8192]{1,0:T(8,128)(2,1)}, bf16[64,8192]{1,0:T(8,128)(2,1)}, ...) | async-done | bytes 4194320 | tf_op jit(solution)/shard_map/psum | solution.py:32
  179.8 3.8 %fusion.3 = bf16[1,8,8,8192]{3,2,0,1:T(8,128)(2,1)} fusion(bf16[64,8192]{1,0:T(8,128)(2,1)} %get-tuple-element.5, bf16[8,8,8192]{2,1,0:T(8,128)(2,1)S(1)} %gather_fusion.1, bf16[64,8192]{1,0:T(8,128)(2,1)} %get-tuple-element.6), kind=kOutput, calls=%fused_computation.9 | convolution fusion | flops 134746112 | bytes 4194304 | tf_op jit(solution)/shard_map/scnr,srd->scnd/dot_general | solution.py:48
  183.6 3.7 %all-to-all-start.1 = ((bf16[1,8,8,8192]{3,2,0,1:T(8,128)(2,1)}), bf16[1,8,8,8192]{3,2,0,1:T(8,128)(2,1)S(1)}, u32[]{:S(2)}, u32[]{:S(2)}) async-start(bf16[1,8,8,8192]{3,2,0,1:T(8,128)(2,1)} %fusion.3), calls=%async_computation.1 | async-start | bytes 2097152 | tf_op jit(solution)/shard_map/all_to_all | solution.py:55
  188.0 3.8 %fusion.1 = bf16[1,8,8,8192]{3,2,0,1:T(8,128)(2,1)} fusion(bf16[64,8192]{1,0:T(8,128)(2,1)} %get-tuple-element.7, bf16[8,8,8192]{2,1,0:T(8,128)(2,1)S(1)} %gather_fusion, bf16[64,8192]{1,0:T(8,128)(2,1)} %get-tuple-element.8), kind=kOutput, calls=%fused_computation.7 | convolution fusion | flops 134746112 | bytes 4194304 | tf_op jit(solution)/shard_map/scnr,srd->scnd/dot_general | solution.py:48
  191.8 10.9 %all-to-all-done.1 = bf16[1,8,8,8192]{3,2,0,1:T(8,128)(2,1)S(1)} async-done(((bf16[1,8,8,8192]{3,2,0,1:T(8,128)(2,1)}), bf16[1,8,8,8192]{3,2,0,1:T(8,128)(2,1)S(1)}, u32[]{:S(2)}, u32[]{:S(2)}) %all-to-all-start.1) | async-done | bytes 1048608 | tf_op jit(solution)/shard_map/all_to_all | solution.py:55
  202.7 3.6 %all-to-all-start = ((bf16[1,8,8,8192]{3,2,0,1:T(8,128)(2,1)}), bf16[1,8,8,8192]{3,2,0,1:T(8,128)(2,1)S(1)}, u32[]{:S(2)}, u32[]{:S(2)}) async-start(bf16[1,8,8,8192]{3,2,0,1:T(8,128)(2,1)} %fusion.1), calls=%async_computation | async-start | bytes 2097152 | tf_op jit(solution)/shard_map/all_to_all | solution.py:55
  206.7 15.0 %all-to-all-done = bf16[1,8,8,8192]{3,2,0,1:T(8,128)(2,1)S(1)} async-done(((bf16[1,8,8,8192]{3,2,0,1:T(8,128)(2,1)}), bf16[1,8,8,8192]{3,2,0,1:T(8,128)(2,1)S(1)}, u32[]{:S(2)}, u32[]{:S(2)}) %all-to-all-start) | async-done | bytes 1048608 | tf_op jit(solution)/shard_map/all_to_all | solution.py:55
  222.0 1.1 pad_maximum_fusion
  (53 shorter events, 8.6 us)
Async XLA Ops:
  6.5 173.3 %all-reduce.3.cloned.1.call-start = ((), (), s32[]{:S(2)}) async-start(), calls=%async_computation.2 | async-start | bytes 8388608 | tf_op jit(solution)/shard_map/psum | solution.py:32
  10.0 6.9 %copy-start.2 = (s32[2,8]{1,0:T(2,128)S(1)}, s32[2,8]{1,0:T(2,128)}, u32[]{:S(2)}) copy-start(s32[2,8]{1,0:T(2,128)} %param.9) | copy-start | bytes 196
  10.0 8.9 %copy-start.1 = (bf16[1,64,8192]{2,1,0:T(8,128)(2,1)S(1)}, bf16[1,64,8192]{2,1,0:T(8,128)(2,1)}, u32[]{:S(2)}) copy-start(bf16[1,64,8192]{2,1,0:T(8,128)(2,1)} %param.8) | copy-start | bytes 3145732
  10.9 13.8 %collective-permute-start.7 = (bf16[1,1,8,8192]{3,2,1,0:T(8,128)(2,1)}, bf16[1,1,8,8192]{3,2,1,0:T(8,128)(2,1)}, u32[]{:S(2)}, u32[]{:S(2)}) collective-permute-start(bf16[1,1,8,8192]{3,2,1,0:T(8,128)(2,1)} %get-tuple-element.23), channel_id=1, source_target_pairs={{0,1},{1,2},{2,3},{3,4},{4,5},{5,6},{6,7},{7,0},{8,9},{9,10},{10,1... | collective-permute-start | bytes 393224 | tf_op jit(solution)/shard_map/ppermute | solution.py:25
  11.3 15.8 %collective-permute-start.8 = (bf16[1,1,8,8192]{3,2,1,0:T(8,128)(2,1)}, bf16[1,1,8,8192]{3,2,1,0:T(8,128)(2,1)}, u32[]{:S(2)}, u32[]{:S(2)}) collective-permute-start(bf16[1,1,8,8192]{3,2,1,0:T(8,128)(2,1)} %get-tuple-element.22), channel_id=1, source_target_pairs={{0,2},{1,3},{2,4},{3,5},{4,6},{5,7},{6,0},{7,1},{8,10},{9,11},{10,... | collective-permute-start | bytes 393224 | tf_op jit(solution)/shard_map/ppermute | solution.py:25
  13.9 16.6 %collective-permute-start.9 = (bf16[1,1,8,8192]{3,2,1,0:T(8,128)(2,1)}, bf16[1,1,8,8192]{3,2,1,0:T(8,128)(2,1)S(1)}, u32[]{:S(2)}, u32[]{:S(2)}) collective-permute-start(bf16[1,1,8,8192]{3,2,1,0:T(8,128)(2,1)} %get-tuple-element.21), channel_id=1, source_target_pairs={{0,3},{1,4},{2,5},{3,6},{4,7},{5,0},{6,1},{7,2},{8,11},{9,12},{10,... | collective-permute-start | bytes 393224 | tf_op jit(solution)/shard_map/ppermute | solution.py:25
  16.2 14.3 %collective-permute-start.10 = (bf16[1,1,8,8192]{3,2,1,0:T(8,128)(2,1)}, bf16[1,1,8,8192]{3,2,1,0:T(8,128)(2,1)S(1)}, u32[]{:S(2)}, u32[]{:S(2)}) collective-permute-start(bf16[1,1,8,8192]{3,2,1,0:T(8,128)(2,1)} %get-tuple-element.20), channel_id=1, source_target_pairs={{0,4},{1,5},{2,6},{3,7},{4,0},{5,1},{6,2},{7,3},{8,12},{9,13},{10,... | collective-permute-start | bytes 393224 | tf_op jit(solution)/shard_map/ppermute | solution.py:25
  16.7 14.5 %collective-permute-start.11 = (bf16[1,1,8,8192]{3,2,1,0:T(8,128)(2,1)}, bf16[1,1,8,8192]{3,2,1,0:T(8,128)(2,1)S(1)}, u32[]{:S(2)}, u32[]{:S(2)}) collective-permute-start(bf16[1,1,8,8192]{3,2,1,0:T(8,128)(2,1)} %get-tuple-element.19), channel_id=1, source_target_pairs={{0,5},{1,6},{2,7},{3,0},{4,1},{5,2},{6,3},{7,4},{8,13},{9,14},{10,... | collective-permute-start | bytes 393224 | tf_op jit(solution)/shard_map/ppermute | solution.py:25
  22.2 1.2 copy-start
  24.7 7.9 %collective-permute-start.12 = (bf16[1,1,8,8192]{3,2,1,0:T(8,128)(2,1)S(1)}, bf16[1,1,8,8192]{3,2,1,0:T(8,128)(2,1)S(1)}, u32[]{:S(2)}, u32[]{:S(2)}) collective-permute-start(bf16[1,1,8,8192]{3,2,1,0:T(8,128)(2,1)S(1)} %get-tuple-element.18), channel_id=1, source_target_pairs={{0,6},{1,7},{2,0},{3,1},{4,2},{5,3},{6,4},{7,5},{8,14},{9,15},{10,... | collective-permute-start | bytes 393224 | tf_op jit(solution)/shard_map/ppermute | solution.py:25
  27.1 7.2 %collective-permute-start.13 = (bf16[1,1,8,8192]{3,2,1,0:T(8,128)(2,1)S(1)}, bf16[1,1,8,8192]{3,2,1,0:T(8,128)(2,1)S(1)}, u32[]{:S(2)}, u32[]{:S(2)}) collective-permute-start(bf16[1,1,8,8192]{3,2,1,0:T(8,128)(2,1)S(1)} %get-tuple-element.17), channel_id=1, source_target_pairs={{0,7},{1,0},{2,1},{3,2},{4,3},{5,4},{6,5},{7,6},{8,15},{9,8},{10,9... | collective-permute-start | bytes 393224 | tf_op jit(solution)/shard_map/ppermute | solution.py:25
  30.5 6.2 %collective-permute-start = (bf16[1,1,8,8192]{3,2,1,0:T(8,128)(2,1)S(1)}, bf16[1,1,8,8192]{3,2,1,0:T(8,128)(2,1)S(1)}, u32[]{:S(2)}, u32[]{:S(2)}) collective-permute-start(bf16[1,1,8,8192]{3,2,1,0:T(8,128)(2,1)S(1)} %get-tuple-element.15), channel_id=1, source_target_pairs={{0,1},{1,2},{2,3},{3,4},{4,5},{5,6},{6,7},{7,0},{8,9},{9,10},{10,1... | collective-permute-start | bytes 393224 | tf_op jit(solution)/shard_map/ppermute | solution.py:25
  30.6 7.4 %collective-permute-start.1 = (bf16[1,1,8,8192]{3,2,1,0:T(8,128)(2,1)S(1)}, bf16[1,1,8,8192]{3,2,1,0:T(8,128)(2,1)S(1)}, u32[]{:S(2)}, u32[]{:S(2)}) collective-permute-start(bf16[1,1,8,8192]{3,2,1,0:T(8,128)(2,1)S(1)} %get-tuple-element.14), channel_id=1, source_target_pairs={{0,2},{1,3},{2,4},{3,5},{4,6},{5,7},{6,0},{7,1},{8,10},{9,11},{10,... | collective-permute-start | bytes 393224 | tf_op jit(solution)/shard_map/ppermute | solution.py:25
  31.2 11.5 %collective-permute-start.2 = (bf16[1,1,8,8192]{3,2,1,0:T(8,128)(2,1)S(1)}, bf16[1,1,8,8192]{3,2,1,0:T(8,128)(2,1)S(1)}, u32[]{:S(2)}, u32[]{:S(2)}) collective-permute-start(bf16[1,1,8,8192]{3,2,1,0:T(8,128)(2,1)S(1)} %get-tuple-element.13), channel_id=1, source_target_pairs={{0,3},{1,4},{2,5},{3,6},{4,7},{5,0},{6,1},{7,2},{8,11},{9,12},{10,... | collective-permute-start | bytes 393224 | tf_op jit(solution)/shard_map/ppermute | solution.py:25
  32.7 10.3 %collective-permute-start.3 = (bf16[1,1,8,8192]{3,2,1,0:T(8,128)(2,1)S(1)}, bf16[1,1,8,8192]{3,2,1,0:T(8,128)(2,1)S(1)}, u32[]{:S(2)}, u32[]{:S(2)}) collective-permute-start(bf16[1,1,8,8192]{3,2,1,0:T(8,128)(2,1)S(1)} %get-tuple-element.12), channel_id=1, source_target_pairs={{0,4},{1,5},{2,6},{3,7},{4,0},{5,1},{6,2},{7,3},{8,12},{9,13},{10,... | collective-permute-start | bytes 393224 | tf_op jit(solution)/shard_map/ppermute | solution.py:25
  34.3 9.2 %collective-permute-start.4 = (bf16[1,1,8,8192]{3,2,1,0:T(8,128)(2,1)S(1)}, bf16[1,1,8,8192]{3,2,1,0:T(8,128)(2,1)S(1)}, u32[]{:S(2)}, u32[]{:S(2)}) collective-permute-start(bf16[1,1,8,8192]{3,2,1,0:T(8,128)(2,1)S(1)} %get-tuple-element.11), channel_id=1, source_target_pairs={{0,5},{1,6},{2,7},{3,0},{4,1},{5,2},{6,3},{7,4},{8,13},{9,14},{10,... | collective-permute-start | bytes 393224 | tf_op jit(solution)/shard_map/ppermute | solution.py:25
  36.7 7.4 %collective-permute-start.5 = (bf16[1,1,8,8192]{3,2,1,0:T(8,128)(2,1)}, bf16[1,1,8,8192]{3,2,1,0:T(8,128)(2,1)S(1)}, u32[]{:S(2)}, u32[]{:S(2)}) collective-permute-start(bf16[1,1,8,8192]{3,2,1,0:T(8,128)(2,1)} %get-tuple-element.10), channel_id=1, source_target_pairs={{0,6},{1,7},{2,0},{3,1},{4,2},{5,3},{6,4},{7,5},{8,14},{9,15},{10,... | collective-permute-start | bytes 393224 | tf_op jit(solution)/shard_map/ppermute | solution.py:25
  38.0 149.4 %collective-permute-start.6 = (bf16[1,1,8,8192]{3,2,1,0:T(8,128)(2,1)S(1)}, bf16[1,1,8,8192]{3,2,1,0:T(8,128)(2,1)S(1)}, u32[]{:S(2)}, u32[]{:S(2)}) collective-permute-start(bf16[1,1,8,8192]{3,2,1,0:T(8,128)(2,1)S(1)} %get-tuple-element.9), channel_id=1, source_target_pairs={{0,7},{1,0},{2,1},{3,2},{4,3},{5,4},{6,5},{7,6},{8,15},{9,8},{10,9... | collective-permute-start | bytes 393224 | tf_op jit(solution)/shard_map/ppermute | solution.py:25
  183.6 19.1 %all-to-all-start.1 = ((bf16[1,8,8,8192]{3,2,0,1:T(8,128)(2,1)}), bf16[1,8,8,8192]{3,2,0,1:T(8,128)(2,1)S(1)}, u32[]{:S(2)}, u32[]{:S(2)}) async-start(bf16[1,8,8,8192]{3,2,0,1:T(8,128)(2,1)} %fusion.3), calls=%async_computation.1 | async-start | bytes 2097152 | tf_op jit(solution)/shard_map/all_to_all | solution.py:55
  202.7 18.9 %all-to-all-start = ((bf16[1,8,8,8192]{3,2,0,1:T(8,128)(2,1)}), bf16[1,8,8,8192]{3,2,0,1:T(8,128)(2,1)S(1)}, u32[]{:S(2)}, u32[]{:S(2)}) async-start(bf16[1,8,8,8192]{3,2,0,1:T(8,128)(2,1)} %fusion.1), calls=%async_computation | async-start | bytes 2097152 | tf_op jit(solution)/shard_map/all_to_all | solution.py:55
Sparse Core Ops, SparseCore 0:
  22.3 157.4 all-reduce.2
